TPU v7x, 32 devices: a whole 2x2x4 slice. The times are simulated.
32 devices in a mesh: grp: 2 (over y), row: 4 (over x, core), col: 4 (over z).
Axes of the slice: x: 2, y: 2, z: 4, core: 2. Of those that a mesh axis runs over, the one named last changes fastest.
Arguments:
- factor: float32 [8, 4, 768, 768], P(('grp', 'row'), 'col'), parts along dimension 0
- rhs: float32 [8, 768, 64], P(('grp', 'row')), parts along dimension 0, may hold values from -6 to 6
- pattern: int32 [8, 4], P('grp'), parts along dimension 0, may hold values from 0 to 1, as said below
Outputs:
- solution: float32 [8, 768, 64], P(('grp', 'col'), 'row'), parts along dimension 0
There are 2 independent parts, one for each index of `grp`. A program takes and returns all parts, laid end to end along the dimension named above; each array names one. Nothing has to cross between parts.
Inputs may be any that keep to these rules, and one draw needn't show every extreme that they name: pattern[i, j] = 1 only where j < i; the blocks form an elimination tree in which every block but the last has exactly one parent p > j with pattern[p, j] = 1, and pattern[i, j] = 1 only where i is an ancestor of j; every chain of blocks linked by pattern has at most 4 blocks and some chain has exactly 4.
All inputs are finite; a program needn't handle non-finite values.
Results may differ from a plain program's by a relative error of at most 0.0001.
Values sent between devices are 32-bit elements; how exact they have to be, the bound alone decides.
A program may use at most 64 MiB of HBM per device.

v0:
```python
import jax
import jax.numpy as jnp
from jax import lax
from jax.sharding import PartitionSpec as P


def from_root(shard, axis, root):
    mine = lax.axis_index(axis) == root
    return lax.psum(jnp.where(mine, shard, jnp.zeros_like(shard)), axis)


def multiply(factor_tile, columns):
    return jnp.dot(
        factor_tile, columns, precision=lax.Precision.HIGHEST, preferred_element_type=jnp.float32
    )


def advance(factor_tile, right_cols, carried, solve_now, apply_now, final_level):

    def solve_branch(operand):
        return multiply(factor_tile, operand)

    def empty_branch(operand):
        return jnp.zeros_like(operand)

    fresh = lax.cond(solve_now, solve_branch, empty_branch, right_cols - carried)
    arrived = from_root(fresh, "row", lax.axis_index("col"))
    if not final_level:
        product = lax.cond(apply_now, solve_branch, empty_branch, arrived)
        carried = carried + lax.psum(product, "col")
    return (arrived, carried)


def local(factor, rhs, pattern):
    factor_tile = factor[0, 0]
    right_rows = rhs[0]
    here_row = lax.axis_index("row")
    here_col = lax.axis_index("col")
    depth_count = min(6, lax.axis_size("row"))
    linked = pattern == 1
    height = jnp.zeros((pattern.shape[0],), jnp.int32)
    for sweep_index in range(depth_count):
        height = jnp.max(jnp.where(linked, height[None, :] + 1, 0), axis=1)
    own_height = height[here_row]
    column_height = height[here_col]
    on_diagonal = here_row == here_col
    uses_block = pattern[here_row, here_col] == 1
    pieces = [right_rows]
    carried = [jnp.zeros_like(piece) for piece in pieces]
    solved = [jnp.zeros_like(piece) for piece in pieces]
    for level_now in range(depth_count):
        solve_now = on_diagonal & (own_height == level_now)
        apply_now = uses_block & (column_height == level_now)
        arrived, carried[0] = advance(
            factor_tile, pieces[0], carried[0], solve_now, apply_now, level_now == depth_count - 1
        )
        solved[0] = solved[0] + arrived
    solved_all = solved[0]
    own_rows = solved_all.shape[0] // lax.axis_size("row")
    return lax.dynamic_slice_in_dim(solved_all, here_row * own_rows, own_rows, 0)[None]


def solution(mesh):
    in_specs = (P(("grp", "row"), "col", None, None), P(("grp", "row"), None, None), P("grp", None))
    out_specs = P(("grp", "col"), "row", None)
    return jax.shard_map(local, mesh=mesh, in_specs=in_specs, out_specs=out_specs, check_vma=False)
```

profile of v0, /device:TPU:29, one launch (start us, length us, event | category | flops | bytes accessed | tf_op | source)
XLA Modules:
  0.0 275.2 jit_solution(16955222185634692702)
XLA Ops:
  6.5 0.8 select_reduce_fusion.3
  7.3 0.1 select_reduce_fusion.2
  7.5 0.1 select_reduce_fusion.1
  7.6 0.1 select_reduce_fusion
  7.7 0.6 fusion.5
  9.0 1.1 copy.4
  10.1 0.7 broadcast_select_fusion.3
  10.9 1.3 dynamic_slice.13
  13.4 29.1 %all-reduce.8.cloned.1.call-done = f32[768,64]{0,1:T(8,128)} async-done(((f32[768,64]{0,1:T(8,128)}), f32[768,64]{0,1:T(8,128)}) %all-reduce.8.cloned.1.call-update) | async-done | bytes 196624 | tf_op jit(solution)/shard_map/psum | solution.py:9
  42.5 0.9 copy.6
  44.2 35.7 %all-reduce.10.cloned.1.call-done = f32[768,64]{1,0:T(8,128)} async-done(((f32[768,64]{1,0:T(8,128)}), f32[768,64]{1,0:T(8,128)}) %all-reduce.10.cloned.1.call-update) | async-done | bytes 196624 | tf_op jit(solution)/shard_map/psum | solution.py:30
  79.9 0.7 broadcast_select_fusion.2
  81.3 34.4 %all-reduce.12.cloned.1.call-done = f32[768,64]{0,1:T(8,128)} async-done(((f32[768,64]{0,1:T(8,128)}), f32[768,64]{0,1:T(8,128)}) %all-reduce.12.cloned.1.call-update) | async-done | bytes 196624 | tf_op jit(solution)/shard_map/psum | solution.py:9
  115.8 0.9 copy.8
  117.4 36.4 %all-reduce.14.cloned.1.call-done = f32[768,64]{1,0:T(8,128)} async-done(((f32[768,64]{1,0:T(8,128)}), f32[768,64]{1,0:T(8,128)}) %all-reduce.14.cloned.1.call-update) | async-done | bytes 196624 | tf_op jit(solution)/shard_map/psum | solution.py:30
  153.8 1.0 add.71
  154.9 0.7 broadcast_select_fusion.1
  156.3 36.6 %all-reduce.16.cloned.1.call-done = f32[768,64]{0,1:T(8,128)} async-done(((f32[768,64]{0,1:T(8,128)}), f32[768,64]{0,1:T(8,128)}) %all-reduce.16.cloned.1.call-update) | async-done | bytes 196624 | tf_op jit(solution)/shard_map/psum | solution.py:9
  192.9 0.2 conditional.12
  193.1 0.9 copy.10
  194.7 35.9 %all-reduce.18.cloned.1.call-done = f32[768,64]{1,0:T(8,128)} async-done(((f32[768,64]{1,0:T(8,128)}), f32[768,64]{1,0:T(8,128)}) %all-reduce.18.cloned.1.call-update) | async-done | bytes 196624 | tf_op jit(solution)/shard_map/psum | solution.py:30
  230.7 0.7 broadcast_select_fusion
  231.4 35.1 %all-reduce.20.cloned.1.call-done = f32[768,64]{0,1:T(8,128)} async-done(((f32[768,64]{0,1:T(8,128)}), f32[768,64]{0,1:T(8,128)}) %all-reduce.20.cloned.1.call-update) | async-done | bytes 196624 | tf_op jit(solution)/shard_map/psum | solution.py:9
  266.5 1.8 fusion.4
  (32 shorter events, 0.6 us)
Async XLA Ops:
  6.5 36.0 %all-reduce.8.cloned.1.call-start = ((), (), s32[]{:S(2)}) async-start(), calls=%async_computation | async-start | bytes 393216 | tf_op jit(solution)/shard_map/psum | solution.py:9
  10.8 69.1 %all-reduce.10.cloned.1.call-start = ((), (), s32[]{:S(2)}) async-start(), calls=%async_computation.1 | async-start | bytes 786432 | tf_op jit(solution)/shard_map/psum | solution.py:30
  43.5 72.2 %all-reduce.12.cloned.1.call-start = ((), (), s32[]{:S(2)}) async-start(), calls=%async_computation.2 | async-start | bytes 393216 | tf_op jit(solution)/shard_map/psum | solution.py:9
  79.9 73.9 %copy-start = (f32[768,64]{1,0:T(8,128)S(1)}, f32[768,64]{1,0:T(8,128)}, u32[]{:S(2)}) copy-start(f32[768,64]{1,0:T(8,128)} %all-reduce.10.cloned.1.call-done) | copy-start | bytes 589828
  80.6 73.1 %all-reduce.14.cloned.1.call-start = ((), (), s32[]{:S(2)}) async-start(), calls=%async_computation.3 | async-start | bytes 786432 | tf_op jit(solution)/shard_map/psum | solution.py:30
  116.7 76.2 %all-reduce.16.cloned.1.call-start = ((), (), s32[]{:S(2)}) async-start(), calls=%async_computation.4 | async-start | bytes 393216 | tf_op jit(solution)/shard_map/psum | solution.py:9
  155.6 75.0 %all-reduce.18.cloned.1.call-start = ((), (), s32[]{:S(2)}) async-start(), calls=%async_computation.5 | async-start | bytes 786432 | tf_op jit(solution)/shard_map/psum | solution.py:30
  194.1 72.5 %all-reduce.20.cloned.1.call-start = ((), (), s32[]{:S(2)}) async-start(), calls=%async_computation.6 | async-start | bytes 393216 | tf_op jit(solution)/shard_map/psum | solution.py:9
Sparse Core Ops, SparseCore 0:
  10.9 31.5 all-reduce.7
  45.0 34.8 all-reduce.9
  82.2 33.4 all-reduce.11
  118.1 35.6 all-reduce.13
  156.0 36.8 all-reduce.15
  195.2 35.3 all-reduce.17
  233.0 33.5 all-reduce.19
where the time goes:
time: 278 us; the launch traced here: 275 us
  waiting for transfers between devices  243 us (87%)
  between operations  18.7 us (7%)
  other arithmetic  6.79 us (2%)
  local copies, waits for them, and re-layouts  5.86 us (2%)
    psum x4, waiting for transfers between devices, from_root(): return lax.psum(jnp.where(mine, shard, jnp.zeros_like(shard)), axis)  135 us
    psum x3, waiting for transfers between devices, advance(): carried = carried + lax.psum(product, 'col')  108 us
  transfers between devices with their start and end apart: 7, of which 7 were waited for; matrix products, arithmetic and copies ran while one was open for 0% of the time, Pallas kernels for 0%

commit v1 on v0

v1 whole, which is shorter than its diff:
```python
import functools

import jax
import jax.numpy as jnp
from jax import lax
from jax.experimental import pallas as pl
from jax.experimental.pallas import tpu as pltpu
from jax.sharding import PartitionSpec as P

MESH = pl.DeviceIdType.MESH
BF = jnp.bfloat16
F32 = jnp.float32


def low_lanes(shape, half):
    return lax.broadcasted_iota(jnp.int32, shape, 1) < half


def halves(packed, half):
    low = low_lanes(packed.shape, half)
    lead = packed.astype(BF).astype(F32)
    rest = packed - lead
    upper = jnp.where(low, lead, pltpu.roll(rest, half, 1))
    lower = jnp.where(low, pltpu.roll(lead, half, 1), rest)
    return upper.astype(BF), lower.astype(BF)


def kernel(
    n, size, step, half,
    factor, rhs, pattern, out,
    a32, ahi, alo, right, w, acc, both, sent, xin, pin, piece, pin_slice,
    a_sem, r_sem, x_send, x_recv, p_send, p_recv, s_send, s_recv,
):
    r = lax.axis_index("row")
    c = lax.axis_index("col")
    chunks = size // step
    mid = step // 2
    own = size // n
    bit = own // 2
    diag = r == c
    lower = r > c
    active = r >= c

    def load(k):
        rows = pl.ds(k * step, step)
        return pltpu.make_async_copy(factor.at[0, 0, rows, :], a32.at[rows, :], a_sem.at[k])

    def load_right():
        return pltpu.make_async_copy(rhs.at[0], right, r_sem)

    @pl.when(active)
    def _():
        for k in range(chunks):
            load(k).start()

    @pl.when(diag)
    def _():
        load_right().start()

    barrier = pltpu.get_barrier_semaphore()
    for i in range(n):
        @pl.when(diag & (i < r))
        def _():
            pl.semaphore_signal(barrier, inc=1, device_id={"col": i}, device_id_type=MESH)

    @pl.when(jnp.logical_not(diag))
    def _():
        pl.semaphore_signal(barrier, inc=1, device_id={"row": c}, device_id_type=MESH)

    @pl.when(active)
    def _():
        keep = jnp.where(diag | (pattern[r, c] == 1), 1.0, 0.0).astype(F32)
        block = 64
        for k in range(chunks):
            load(k).wait()

            def split(t, carry):
                rows = pl.ds(pl.multiple_of(k * step + t * block, block), block)
                full = a32[rows, :] * keep
                lead = full.astype(BF)
                ahi[rows, :] = lead
                alo[rows, :] = (full - lead.astype(F32)).astype(BF)
                return carry

            lax.fori_loop(0, step // block, split, 0)

    @pl.when(diag)
    def _():
        load_right().wait()
        pl.semaphore_wait(barrier, n - 1)

    @pl.when(lower)
    def _():
        pl.semaphore_wait(barrier, 1)

    def x_copy(i, m):
        return pltpu.make_async_remote_copy(
            src_ref=sent.at[m], dst_ref=xin.at[m], send_sem=x_send.at[i, m], recv_sem=x_recv.at[m],
            device_id={"row": i}, device_id_type=MESH,
        )

    def p_copy(m):
        return pltpu.make_async_remote_copy(
            src_ref=sent.at[m], dst_ref=pin.at[c, m], send_sem=p_send.at[m], recv_sem=p_recv.at[c, m],
            device_id={"col": r}, device_id_type=MESH,
        )

    def p_arrival(j, m):
        return pltpu.make_async_remote_copy(
            src_ref=sent.at[m], dst_ref=pin.at[j, m], send_sem=p_send.at[m], recv_sem=p_recv.at[j, m],
            device_id={"col": r}, device_id_type=MESH,
        )

    def s_copy(i):
        return pltpu.make_async_remote_copy(
            src_ref=piece.at[i], dst_ref=pin_slice, send_sem=s_send.at[i], recv_sem=s_recv,
            device_id={"row": i}, device_id_type=MESH,
        )

    def place(value):
        out[0, :bit, :] = value[:, :half]
        out[0, bit:, :] = pltpu.roll(value, half, 1)[:, :half]

    @pl.when(diag)
    def _():
        for k in range(chunks):
            base = k * step
            xin[k] = jnp.concatenate(
                [right[base:base + mid, :], right[base + mid:base + step, :]], axis=1
            )

    @pl.when(active)
    def _():
        for k in range(chunks):
            base = k * step

            @pl.when(lower)
            def _():
                x_copy(0, k).wait_recv()

            for j in range(n - 1):
                @pl.when(diag & (j < r))
                def _():
                    p_arrival(j, k).wait_recv()
                    xin[k] = xin[k] - pin[j, k]

            first, second = halves(xin[k], half)
            w[base:base + mid, :] = first
            w[base + mid:base + step, :] = second
            last = k == chunks - 1
            for m in range(chunks):
                rows = slice(m * step, (m + 1) * step)
                cols = slice(base, base + step)
                part = jnp.dot(ahi[rows, cols], w[cols, :], preferred_element_type=F32)
                part += jnp.dot(alo[rows, cols], w[cols, :], preferred_element_type=F32)
                if k:
                    part += acc[rows, :]
                if not last:
                    acc[rows, :] = part
                    continue
                part = part + pltpu.roll(part, half, 1)
                both[rows, :] = part
                sent[m] = jnp.where(low_lanes((mid, 2 * half), half), part[:mid], part[mid:])

                @pl.when(lower)
                def _():
                    p_copy(m).start()

                for i in range(1, n):
                    @pl.when(diag & (i > r))
                    def _():
                        x_copy(i, m).start()

    @pl.when(diag)
    def _():
        for i in range(n):
            top = both[i * own:i * own + bit, :]
            bottom = both[i * own + bit:(i + 1) * own, :]
            value = jnp.where(low_lanes((bit, 2 * half), half), top, bottom)
            piece[i] = value

            @pl.when(i != r)
            def _():
                s_copy(i).start()

            @pl.when(i == r)
            def _():
                place(value)

    @pl.when(jnp.logical_not(diag))
    def _():
        s_copy(0).wait_recv()
        place(pin_slice[...])

    @pl.when(lower)
    def _():
        for m in range(chunks):
            p_copy(m).wait_send()

    for i in range(n):
        @pl.when(diag & (i > r))
        def _():
            for m in range(chunks):
                x_copy(i, m).wait_send()

        @pl.when(diag & (i != r))
        def _():
            s_copy(i).wait_send()


def local(n, factor, rhs, pattern):
    size, columns = rhs.shape[1], rhs.shape[2]
    step = 256 if size % 256 == 0 else size
    chunks = size // step
    half = columns
    own = size // n
    dma = pltpu.SemaphoreType.DMA
    return pl.pallas_call(
        functools.partial(kernel, n, size, step, half),
        out_shape=jax.ShapeDtypeStruct((1, own, columns), F32),
        in_specs=[
            pl.BlockSpec(memory_space=pl.ANY),
            pl.BlockSpec(memory_space=pl.ANY),
            pl.BlockSpec(memory_space=pltpu.SMEM),
        ],
        out_specs=pl.BlockSpec(memory_space=pltpu.VMEM),
        scratch_shapes=[
            pltpu.VMEM((size, size), F32),
            pltpu.VMEM((size, size), BF),
            pltpu.VMEM((size, size), BF),
            pltpu.VMEM((size, columns), F32),
            pltpu.VMEM((size, 2 * half), BF),
            pltpu.VMEM((size, 2 * half), F32),
            pltpu.VMEM((size, 2 * half), F32),
            pltpu.VMEM((chunks, step // 2, 2 * half), F32),
            pltpu.VMEM((chunks, step // 2, 2 * half), F32),
            pltpu.VMEM((n - 1, chunks, step // 2, 2 * half), F32),
            pltpu.VMEM((n, own // 2, 2 * half), F32),
            pltpu.VMEM((own // 2, 2 * half), F32),
            dma((chunks,)),
            dma,
            dma((n, chunks)),
            dma((chunks,)),
            dma((chunks,)),
            dma((n - 1, chunks)),
            dma((n,)),
            dma,
        ],
        compiler_params=pltpu.CompilerParams(
            collective_id=0, has_side_effects=True, vmem_limit_bytes=40 * 1024 * 1024
        ),
    )(factor, rhs, pattern)


def solution(mesh):
    in_specs = (P(("grp", "row"), "col", None, None), P(("grp", "row"), None, None), P("grp", None))
    out_specs = P(("grp", "col"), "row", None)
    return jax.shard_map(
        functools.partial(local, mesh.shape["row"]),
        mesh=mesh, in_specs=in_specs, out_specs=out_specs, check_vma=False,
    )
```

time: 278 us -> 36.3 us (0.13)
  waiting for transfers between devices: 243 us -> 0 us
  Pallas kernels: 0 us -> 31.9 us
  between operations: 18.7 us -> 0.02 us
  other arithmetic: 6.79 us -> 0 us
    psum x7 -> x0, waiting for transfers between devices: 243 us -> none  [the longest x4 135 us: from_root(): return lax.psum(jnp.where(mine, shard, jnp.zeros_like(shard)), axis)]
    pallas_call x0 -> x1, Pallas kernels: none -> 31.9 us  [local(): pl.pallas_call(functools.partial(kernel, n, size, step, half), out_shape=...]
  transfers between devices with their start and end apart: 7 -> 0, of which waited for: 7 -> 0; matrix products, arithmetic and copies ran while one was open for 0% -> 0% of each run, Pallas kernels for 0% -> 0%
where the time goes in v1:
time: 36.3 us; the launch traced here: 36.1 us
  Pallas kernels  31.9 us (88%)
  local copies, waits for them, and re-layouts  4.15 us (11%)
    pallas_call x1, Pallas kernels, local(): pl.pallas_call(functools.partial(kernel, n, size, step, half), out_shape=...  31.9 us
    unnamed x5, local copies, waits for them, and re-layouts  3.43 us

profile of v1, /device:TPU:29, one launch (start us, length us, event | category | flops | bytes accessed | tf_op | source)
XLA Modules:
  0.0 36.1 jit_solution(789525531486417303)
XLA Ops:
  0.0 1.1 %copy.4.rhs = f32[1,768,64]{2,1,0:T(8,128)S(1)} copy(f32[1,768,64]{1,2,0:T(8,128)} %param.4) | data formatting | bytes 393216 | tf_op args[1]
  1.1 0.0 copy-start
  1.1 1.7 %copy-done = f32[1,1,768,768]{3,2,1,0:T(8,128)S(1)} copy-done((f32[1,1,768,768]{3,2,1,0:T(8,128)S(1)}, f32[1,1,768,768]{3,2,1,0:T(8,128)}, u32[]{:S(2)}) %copy-start) | copy-done | bytes 2359320
  2.8 0.0 copy-start.1
  2.8 0.7 %copy-done.1 = s32[4,4]{1,0:T(4,128)S(1)} copy-done((s32[4,4]{1,0:T(4,128)S(1)}, s32[4,4]{1,0:T(4,128)}, u32[]{:S(2)}) %copy-start.1) | copy-done | bytes 88
  3.4 31.9 %shard_map.37 = f32[1,192,64]{2,1,0:T(8,128)S(1)} custom-call(f32[1,1,768,768]{3,2,1,0:T(8,128)S(1)} %copy-done, f32[1,768,64]{2,1,0:T(8,128)S(1)} %copy.4.rhs, s32[4,4]{1,0:T(4,128)S(1)} %copy-done.1), custom_call_target="tpu_custom_call" | custom-call | tf_op jit(solution)/shard_map/pallas_call | solution.py:218
  35.4 0.7 %copy.5 = f32[1,192,64]{1,2,0:T(8,128)} copy(f32[1,192,64]{2,1,0:T(8,128)S(1)} %shard_map.37) | data formatting | bytes 98304 | tf_op jit(solution)/shard_map/pallas_call | solution.py:218
Async XLA Ops:
  1.1 1.7 %copy-start = (f32[1,1,768,768]{3,2,1,0:T(8,128)S(1)}, f32[1,1,768,768]{3,2,1,0:T(8,128)}, u32[]{:S(2)}) copy-start(f32[1,1,768,768]{3,2,1,0:T(8,128)} %factor.1) | copy-start | bytes 7077892
  2.8 0.7 %copy-start.1 = (s32[4,4]{1,0:T(4,128)S(1)}, s32[4,4]{1,0:T(4,128)}, u32[]{:S(2)}) copy-start(s32[4,4]{1,0:T(4,128)} %pattern.1) | copy-start | bytes 196

commit v2 on v1

--- a/solution.py
+++ b/solution.py
@@ -28,8 +28,8 @@
 def kernel(
     n, size, step, half,
     factor, rhs, pattern, out,
-    a32, ahi, alo, right, w, acc, both, sent, xin, pin, piece, pin_slice,
-    a_sem, r_sem, x_send, x_recv, p_send, p_recv, s_send, s_recv,
+    links, a32, ahi, alo, right, w, acc, both, sent, xin, pin, piece, pin_slice,
+    a_sem, r_sem, l_sem, x_send, x_recv, p_send, p_recv, s_send, s_recv,
 ):
     r = lax.axis_index("row")
     c = lax.axis_index("col")
@@ -48,14 +48,21 @@
     def load_right():
         return pltpu.make_async_copy(rhs.at[0], right, r_sem)
 
+    def load_links():
+        return pltpu.make_async_copy(pattern, links, l_sem)
+
     @pl.when(active)
     def _():
+        load_links().start()
+
+    @pl.when(diag)
+    def _():
+        load_right().start()
+
+    @pl.when(active)
+    def _():
         for k in range(chunks):
             load(k).start()
-
-    @pl.when(diag)
-    def _():
-        load_right().start()
 
     barrier = pltpu.get_barrier_semaphore()
     for i in range(n):
@@ -67,31 +74,20 @@
     def _():
         pl.semaphore_signal(barrier, inc=1, device_id={"row": c}, device_id_type=MESH)
 
-    @pl.when(active)
-    def _():
-        keep = jnp.where(diag | (pattern[r, c] == 1), 1.0, 0.0).astype(F32)
-        block = 64
-        for k in range(chunks):
-            load(k).wait()
-
-            def split(t, carry):
-                rows = pl.ds(pl.multiple_of(k * step + t * block, block), block)
-                full = a32[rows, :] * keep
-                lead = full.astype(BF)
-                ahi[rows, :] = lead
-                alo[rows, :] = (full - lead.astype(F32)).astype(BF)
-                return carry
-
-            lax.fori_loop(0, step // block, split, 0)
-
-    @pl.when(diag)
-    def _():
-        load_right().wait()
-        pl.semaphore_wait(barrier, n - 1)
-
-    @pl.when(lower)
-    def _():
-        pl.semaphore_wait(barrier, 1)
+    block = 64
+
+    def prepare(k, keep):
+        load(k).wait()
+
+        def split(t, carry):
+            rows = pl.ds(pl.multiple_of(k * step + t * block, block), block)
+            full = a32[rows, :] * keep
+            lead = full.astype(BF)
+            ahi[rows, :] = lead
+            alo[rows, :] = (full - lead.astype(F32)).astype(BF)
+            return carry
+
+        lax.fori_loop(0, step // block, split, 0)
 
     def x_copy(i, m):
         return pltpu.make_async_remote_copy(
@@ -118,19 +114,62 @@
         )
 
     def place(value):
-        out[0, :bit, :] = value[:, :half]
-        out[0, bit:, :] = pltpu.roll(value, half, 1)[:, :half]
+        turned = value.T
+        out[0, :, :bit] = turned[:half]
+        out[0, :, bit:] = turned[half:]
+
+    def weave(k):
+        first, second = halves(xin[k], half)
+        w[k * step:k * step + mid, :] = first
+        w[k * step + mid:(k + 1) * step, :] = second
+
+    def product(rows, cols):
+        part = jnp.dot(ahi[rows, cols], w[cols, :], preferred_element_type=F32)
+        return part + jnp.dot(alo[rows, cols], w[cols, :], preferred_element_type=F32)
+
+    def finish(m, part):
+        part = part + pltpu.roll(part, half, 1)
+        both[m * step:(m + 1) * step, :] = part
+        sent[m] = jnp.where(low_lanes((mid, 2 * half), half), part[:mid], part[mid:])
 
     @pl.when(diag)
     def _():
+        load_right().wait()
         for k in range(chunks):
             base = k * step
             xin[k] = jnp.concatenate(
-                [right[base:base + mid, :], right[base + mid:base + step, :]], axis=1
-            )
+                [right[:, base:base + mid], right[:, base + mid:base + step]], axis=0
+            ).T
 
     @pl.when(active)
     def _():
+        load_links().wait()
+
+    @pl.when(diag & (r == 0))
+    def _():
+        for k in range(chunks):
+            weave(k)
+        for m in range(chunks):
+            prepare(m, jnp.float32(1.0))
+            finish(m, product(slice(m * step, (m + 1) * step), slice(0, size)))
+            if m == 0:
+                pl.semaphore_wait(barrier, n - 1)
+            x_copy(1, m).start()
+
+    @pl.when(active & (r > 0))
+    def _():
+        keep = jnp.where(diag | (links[r, c] == 1), 1.0, 0.0).astype(F32)
+        for k in range(chunks):
+            prepare(k, keep)
+
+        @pl.when(diag)
+        def _():
+            pl.semaphore_wait(barrier, n - 1)
+
+        @pl.when(lower)
+        def _():
+            pl.semaphore_wait(barrier, 1)
+
         for k in range(chunks):
             base = k * step
 
@@ -144,32 +183,32 @@
                     p_arrival(j, k).wait_recv()
                     xin[k] = xin[k] - pin[j, k]
 
-            first, second = halves(xin[k], half)
-            w[base:base + mid, :] = first
-            w[base + mid:base + step, :] = second
+            weave(k)
             last = k == chunks - 1
             for m in range(chunks):
                 rows = slice(m * step, (m + 1) * step)
-                cols = slice(base, base + step)
-                part = jnp.dot(ahi[rows, cols], w[cols, :], preferred_element_type=F32)
-                part += jnp.dot(alo[rows, cols], w[cols, :], preferred_element_type=F32)
+                part = product(rows, slice(base, base + step))
                 if k:
                     part += acc[rows, :]
                 if not last:
                     acc[rows, :] = part
                     continue
-                part = part + pltpu.roll(part, half, 1)
-                both[rows, :] = part
-                sent[m] = jnp.where(low_lanes((mid, 2 * half), half), part[:mid], part[mid:])
+                finish(m, part)
 
                 @pl.when(lower)
                 def _():
                     p_copy(m).start()
 
-                for i in range(1, n):
-                    @pl.when(diag & (i > r))
+                for i in range(2, n):
+                    @pl.when(diag & (i == r + 1))
                     def _():
                         x_copy(i, m).start()
+
+    for i in range(2, n):
+        @pl.when(diag & (i > r + 1))
+        def _():
+            for m in range(chunks):
+                x_copy(i, m).start()
 
     @pl.when(diag)
     def _():
@@ -215,20 +254,21 @@
     half = columns
     own = size // n
     dma = pltpu.SemaphoreType.DMA
-    return pl.pallas_call(
+    solved = pl.pallas_call(
         functools.partial(kernel, n, size, step, half),
-        out_shape=jax.ShapeDtypeStruct((1, own, columns), F32),
+        out_shape=jax.ShapeDtypeStruct((1, columns, own), F32),
         in_specs=[
-            pl.BlockSpec(memory_space=pl.ANY),
-            pl.BlockSpec(memory_space=pl.ANY),
-            pl.BlockSpec(memory_space=pltpu.SMEM),
+            pl.BlockSpec(memory_space=pltpu.HBM),
+            pl.BlockSpec(memory_space=pltpu.HBM),
+            pl.BlockSpec(memory_space=pltpu.HBM),
         ],
         out_specs=pl.BlockSpec(memory_space=pltpu.VMEM),
         scratch_shapes=[
+            pltpu.SMEM(pattern.shape, jnp.int32),
             pltpu.VMEM((size, size), F32),
             pltpu.VMEM((size, size), BF),
             pltpu.VMEM((size, size), BF),
-            pltpu.VMEM((size, columns), F32),
+            pltpu.VMEM((columns, size), F32),
             pltpu.VMEM((size, 2 * half), BF),
             pltpu.VMEM((size, 2 * half), F32),
             pltpu.VMEM((size, 2 * half), F32),
@@ -238,6 +278,7 @@
             pltpu.VMEM((n, own // 2, 2 * half), F32),
             pltpu.VMEM((own // 2, 2 * half), F32),
             dma((chunks,)),
+            dma,
             dma,
             dma((n, chunks)),
             dma((chunks,)),
@@ -249,7 +290,8 @@
         compiler_params=pltpu.CompilerParams(
             collective_id=0, has_side_effects=True, vmem_limit_bytes=40 * 1024 * 1024
         ),
-    )(factor, rhs, pattern)
+    )(*[pltpu.with_memory_space_constraint(v, pltpu.HBM) for v in (factor, jnp.swapaxes(rhs, 1, 2), pattern)])
+    return jnp.swapaxes(solved, 1, 2)
 
 
 def solution(mesh):

time: 36.3 us -> 29.1 us (0.80)
  Pallas kernels: 31.9 us -> 28.3 us
  local copies, waits for them, and re-layouts: 4.15 us -> 0.63 us
    pallas_call x1, Pallas kernels: 31.9 us -> 28.3 us  [local(): pl.pallas_call(functools.partial(kernel, n, size, step, half), out_shape=...]
    unnamed x5 -> x1, local copies, waits for them, and re-layouts: 3.43 us -> 0.63 us
    pallas_call x1 -> x0, local copies, waits for them, and re-layouts: 0.71 us -> none  [local(): pl.pallas_call(functools.partial(kernel, n, size, step, half), out_shape=...]
where the time goes in v2:
time: 29.1 us; the launch traced here: 29 us
  Pallas kernels  28.3 us (97%)
  local copies, waits for them, and re-layouts  0.63 us (2%)
    pallas_call x1, Pallas kernels, local(): pl.pallas_call(functools.partial(kernel, n, size, step, half), out_shape=...  28.3 us
    unnamed x1, local copies, waits for them, and re-layouts  0.63 us

profile of v2, /device:TPU:29, one launch (start us, length us, event | category | flops | bytes accessed | tf_op | source)
XLA Modules:
  0.0 29.0 jit_solution(12093474197565403804)
XLA Ops:
  0.0 28.3 %shard_map.37 = f32[1,64,192]{2,1,0:T(8,128)S(1)} custom-call(f32[1,1,768,768]{3,2,1,0:T(8,128)} %factor.1, f32[1,64,768]{2,1,0:T(8,128)} %bitcast.3, s32[4,4]{1,0:T(4,128)} %pattern.1), custom_call_target="tpu_custom_call" | custom-call | tf_op jit(solution)/shard_map/pallas_call | solution.py:257
  28.4 0.6 %copy.5 = f32[1,192,64]{1,2,0:T(8,128)} copy(f32[1,192,64]{1,2,0:T(8,128)S(1)} %bitcast.2) | data formatting | bytes 98304

commit v3 on v2

--- a/solution.py
+++ b/solution.py
@@ -28,8 +28,8 @@
 def kernel(
     n, size, step, half,
     factor, rhs, pattern, out,
-    links, a32, ahi, alo, right, w, acc, both, sent, xin, pin, piece, pin_slice,
-    a_sem, r_sem, l_sem, x_send, x_recv, p_send, p_recv, s_send, s_recv,
+    links, a32, ahi, alo, right, w, acc, both, sent, xin, pin, piece, pin_slice, d32, dhi, dlo,
+    a_sem, r_sem, l_sem, x_send, x_recv, p_send, p_recv, s_send, s_recv, d_send, d_recv, p_send2,
 ):
     r = lax.axis_index("row")
     c = lax.axis_index("col")
@@ -40,6 +40,10 @@
     diag = r == c
     lower = r > c
     active = r >= c
+    helper = (r == n - 1) & (c == n - 2)
+    final = (r == n - 1) & (c == n - 1)
+    early = n // 2
+    from_helper = (c == n - 1) & (r < early)
 
     def load(k):
         rows = pl.ds(k * step, step)
@@ -55,7 +59,7 @@
     def _():
         load_links().start()
 
-    @pl.when(diag)
+    @pl.when(diag | helper)
     def _():
         load_right().start()
 
@@ -70,11 +74,24 @@
         def _():
             pl.semaphore_signal(barrier, inc=1, device_id={"col": i}, device_id_type=MESH)
 
-    @pl.when(jnp.logical_not(diag))
+    @pl.when(jnp.logical_not(diag) & jnp.logical_not(from_helper))
     def _():
         pl.semaphore_signal(barrier, inc=1, device_id={"row": c}, device_id_type=MESH)
 
+    @pl.when(from_helper)
+    def _():
+        pl.semaphore_signal(
+            barrier, inc=1, device_id={"row": n - 1, "col": n - 2}, device_id_type=MESH
+        )
+
+    @pl.when(helper)
+    def _():
+        for j in range(n):
+            if j != n - 2:
+                pl.semaphore_signal(barrier, inc=1, device_id={"col": j}, device_id_type=MESH)
+
     block = 64
+    part_rows = early * own // 2
 
     def prepare(k, keep):
         load(k).wait()
@@ -107,6 +124,26 @@
             device_id={"col": r}, device_id_type=MESH,
         )
 
+    def h_copy(m):
+        return pltpu.make_async_remote_copy(
+            src_ref=sent.at[m], dst_ref=pin.at[c, m], send_sem=p_send2.at[m], recv_sem=p_recv.at[c, m],
+            device_id={"col": n - 2}, device_id_type=MESH,
+        )
+
+    def d_copy(q):
+        rows = pl.ds(q * part_rows, part_rows)
+        return pltpu.make_async_remote_copy(
+            src_ref=factor.at[0, 0, rows, :], dst_ref=d32.at[rows, :],
+            send_sem=d_send.at[q], recv_sem=d_recv.at[q],
+            device_id={"col": n - 2}, device_id_type=MESH,
+        )
+
+    def e_copy(i):
+        return pltpu.make_async_remote_copy(
+            src_ref=piece.at[i], dst_ref=pin_slice, send_sem=s_send.at[i], recv_sem=s_recv,
+            device_id={"row": i, "col": n - 1}, device_id_type=MESH,
+        )
+
     def s_copy(i):
         return pltpu.make_async_remote_copy(
             src_ref=piece.at[i], dst_ref=pin_slice, send_sem=s_send.at[i], recv_sem=s_recv,
@@ -118,8 +155,8 @@
         out[0, :, :bit] = turned[:half]
         out[0, :, bit:] = turned[half:]
 
-    def weave(k):
-        first, second = halves(xin[k], half)
+    def weave(k, value):
+        first, second = halves(value, half)
         w[k * step:k * step + mid, :] = first
         w[k * step + mid:(k + 1) * step, :] = second
 
@@ -132,14 +169,20 @@
         both[m * step:(m + 1) * step, :] = part
         sent[m] = jnp.where(low_lanes((mid, 2 * half), half), part[:mid], part[mid:])
 
+    def right_chunk(k):
+        base = k * step
+        return jnp.concatenate(
+            [right[:, base:base + mid], right[:, base + mid:base + step]], axis=0
+        ).T
+
+    @pl.when(diag | helper)
+    def _():
+        load_right().wait()
+
     @pl.when(diag)
     def _():
-        load_right().wait()
-        for k in range(chunks):
-            base = k * step
-            xin[k] = jnp.concatenate(
-                [right[:, base:base + mid], right[:, base + mid:base + step]], axis=0
-            ).T
+        for k in range(chunks):
+            xin[k] = right_chunk(k)
 
     @pl.when(active)
     def _():
@@ -148,7 +191,7 @@
     @pl.when(diag & (r == 0))
     def _():
         for k in range(chunks):
-            weave(k)
+            weave(k, xin[k])
         for m in range(chunks):
             prepare(m, jnp.float32(1.0))
             finish(m, product(slice(m * step, (m + 1) * step), slice(0, size)))
@@ -159,16 +202,44 @@
     @pl.when(active & (r > 0))
     def _():
         keep = jnp.where(diag | (links[r, c] == 1), 1.0, 0.0).astype(F32)
+
+        @pl.when(final)
+        def _():
+            pl.semaphore_wait(barrier, n - early)
+            for q in range(2):
+                d_copy(q).start()
+
         for k in range(chunks):
             prepare(k, keep)
 
-        @pl.when(diag)
+        @pl.when(diag & (r < n - 1))
         def _():
             pl.semaphore_wait(barrier, n - 1)
 
-        @pl.when(lower)
+        @pl.when(lower & (r < n - 1))
         def _():
             pl.semaphore_wait(barrier, 1)
+
+        @pl.when(lower & (r == n - 1) & (c < n - 2))
+        def _():
+            pl.semaphore_wait(barrier, 2)
+
+        @pl.when(helper)
+        def _():
+            pl.semaphore_wait(barrier, 1 + early)
+            for q in range(2):
+                d_copy(q).wait_recv()
+            strip = 16
+
+            def split(t, carry):
+                rows = pl.ds(pl.multiple_of(t * strip, strip), strip)
+                full = d32[rows, :]
+                lead = full.astype(BF)
+                dhi[rows, :] = lead
+                dlo[rows, :] = (full - lead.astype(F32)).astype(BF)
+                return carry
+
+            lax.fori_loop(0, early * own // strip, split, 0)
 
         for k in range(chunks):
             base = k * step
@@ -183,7 +254,7 @@
                     p_arrival(j, k).wait_recv()
                     xin[k] = xin[k] - pin[j, k]
 
-            weave(k)
+            weave(k, xin[k])
             last = k == chunks - 1
             for m in range(chunks):
                 rows = slice(m * step, (m + 1) * step)
@@ -199,6 +270,10 @@
                 def _():
                     p_copy(m).start()
 
+                @pl.when((r == n - 1) & (c < n - 2))
+                def _():
+                    h_copy(m).start()
+
                 for i in range(2, n):
                     @pl.when(diag & (i == r + 1))
                     def _():
@@ -209,6 +284,22 @@
         def _():
             for m in range(chunks):
                 x_copy(i, m).start()
+
+    @pl.when(helper)
+    def _():
+        for k in range(chunks):
+            value = right_chunk(k) - sent[k]
+            for j in range(n - 2):
+                p_arrival(j, k).wait_recv()
+                value = value - pin[j, k]
+            weave(k, value)
+        for i in range(early):
+            rows = slice(i * own, (i + 1) * own)
+            part = jnp.dot(dhi[rows, :], w[...], preferred_element_type=F32)
+            part += jnp.dot(dlo[rows, :], w[...], preferred_element_type=F32)
+            part = part + pltpu.roll(part, half, 1)
+            piece[i] = jnp.where(low_lanes((bit, 2 * half), half), part[:bit], part[bit:])
+            e_copy(i).start()
 
     @pl.when(diag)
     def _():
@@ -218,7 +309,7 @@
             value = jnp.where(low_lanes((bit, 2 * half), half), top, bottom)
             piece[i] = value
 
-            @pl.when(i != r)
+            @pl.when((i != r) if i >= early else ((i != r) & (r < n - 1)))
             def _():
                 s_copy(i).start()
 
@@ -242,9 +333,24 @@
             for m in range(chunks):
                 x_copy(i, m).wait_send()
 
-        @pl.when(diag & (i != r))
+        @pl.when(diag & ((i != r) if i >= early else ((i != r) & (r < n - 1))))
         def _():
             s_copy(i).wait_send()
+
+    @pl.when((r == n - 1) & (c < n - 2))
+    def _():
+        for m in range(chunks):
+            h_copy(m).wait_send()
+
+    @pl.when(final)
+    def _():
+        for q in range(2):
+            d_copy(q).wait_send()
+
+    @pl.when(helper)
+    def _():
+        for i in range(early):
+            e_copy(i).wait_send()
 
 
 def local(n, factor, rhs, pattern):
@@ -277,6 +383,9 @@
             pltpu.VMEM((n - 1, chunks, step // 2, 2 * half), F32),
             pltpu.VMEM((n, own // 2, 2 * half), F32),
             pltpu.VMEM((own // 2, 2 * half), F32),
+            pltpu.VMEM((n // 2 * own, size), F32),
+            pltpu.VMEM((n // 2 * own, size), BF),
+            pltpu.VMEM((n // 2 * own, size), BF),
             dma((chunks,)),
             dma,
             dma,
@@ -286,6 +395,9 @@
             dma((n - 1, chunks)),
             dma((n,)),
             dma,
+            dma((2,)),
+            dma((2,)),
+            dma((chunks,)),
         ],
         compiler_params=pltpu.CompilerParams(
             collective_id=0, has_side_effects=True, vmem_limit_bytes=40 * 1024 * 1024

time: 29.1 us -> 29.8 us (1.024)
  Pallas kernels: 28.3 us -> 29 us
    pallas_call x1, Pallas kernels: 28.3 us -> 29 us  [local(): pl.pallas_call(functools.partial(kernel, n, size, step, half), out_shape=...]
where the time goes in v3:
time: 29.8 us; the launch traced here: 29.7 us
  Pallas kernels  29 us (97%)
  local copies, waits for them, and re-layouts  0.63 us (2%)
    pallas_call x1, Pallas kernels, local(): pl.pallas_call(functools.partial(kernel, n, size, step, half), out_shape=...  29 us
    unnamed x1, local copies, waits for them, and re-layouts  0.63 us

profile of v3, /device:TPU:29, one launch (start us, length us, event | category | flops | bytes accessed | tf_op | source)
XLA Modules:
  0.0 29.7 jit_solution(9495353882715806600)
XLA Ops:
  0.0 29.0 %shard_map.37 = f32[1,64,192]{2,1,0:T(8,128)S(1)} custom-call(f32[1,1,768,768]{3,2,1,0:T(8,128)} %factor.1, f32[1,64,768]{2,1,0:T(8,128)} %bitcast.3, s32[4,4]{1,0:T(4,128)} %pattern.1), custom_call_target="tpu_custom_call" | custom-call | tf_op jit(solution)/shard_map/pallas_call | solution.py:363
  29.1 0.6 %copy.5 = f32[1,192,64]{1,2,0:T(8,128)} copy(f32[1,192,64]{1,2,0:T(8,128)S(1)} %bitcast.2) | data formatting | bytes 98304

commit v4 on v3

--- a/solution.py
+++ b/solution.py
@@ -29,7 +29,7 @@
     n, size, step, half,
     factor, rhs, pattern, out,
     links, a32, ahi, alo, right, w, acc, both, sent, xin, pin, piece, pin_slice, d32, dhi, dlo,
-    a_sem, r_sem, l_sem, x_send, x_recv, p_send, p_recv, s_send, s_recv, d_send, d_recv, p_send2,
+    a_sem, r_sem, l_sem, x_send, x_recv, p_send, p_recv, s_send, s_recv, d_send, d_recv,
 ):
     r = lax.axis_index("row")
     c = lax.axis_index("col")
@@ -70,7 +70,7 @@
 
     barrier = pltpu.get_barrier_semaphore()
     for i in range(n):
-        @pl.when(diag & (i < r))
+        @pl.when(diag & (i < r) & ((r < n - 1) | (i == n - 2)))
         def _():
             pl.semaphore_signal(barrier, inc=1, device_id={"col": i}, device_id_type=MESH)
 
@@ -115,19 +115,13 @@
     def p_copy(m):
         return pltpu.make_async_remote_copy(
             src_ref=sent.at[m], dst_ref=pin.at[c, m], send_sem=p_send.at[m], recv_sem=p_recv.at[c, m],
-            device_id={"col": r}, device_id_type=MESH,
+            device_id={"col": jnp.where((r == n - 1) & (c < n - 2), n - 2, r)}, device_id_type=MESH,
         )
 
     def p_arrival(j, m):
         return pltpu.make_async_remote_copy(
             src_ref=sent.at[m], dst_ref=pin.at[j, m], send_sem=p_send.at[m], recv_sem=p_recv.at[j, m],
             device_id={"col": r}, device_id_type=MESH,
-        )
-
-    def h_copy(m):
-        return pltpu.make_async_remote_copy(
-            src_ref=sent.at[m], dst_ref=pin.at[c, m], send_sem=p_send2.at[m], recv_sem=p_recv.at[c, m],
-            device_id={"col": n - 2}, device_id_type=MESH,
         )
 
     def d_copy(q):
@@ -216,13 +210,9 @@
         def _():
             pl.semaphore_wait(barrier, n - 1)
 
-        @pl.when(lower & (r < n - 1))
+        @pl.when(lower & jnp.logical_not(helper))
         def _():
             pl.semaphore_wait(barrier, 1)
-
-        @pl.when(lower & (r == n - 1) & (c < n - 2))
-        def _():
-            pl.semaphore_wait(barrier, 2)
 
         @pl.when(helper)
         def _():
@@ -248,11 +238,16 @@
             def _():
                 x_copy(0, k).wait_recv()
 
-            for j in range(n - 1):
-                @pl.when(diag & (j < r))
+            for j in range(n - 2):
+                @pl.when(diag & (j < r) & (r < n - 1))
                 def _():
                     p_arrival(j, k).wait_recv()
                     xin[k] = xin[k] - pin[j, k]
+
+            @pl.when(final)
+            def _():
+                p_arrival(n - 2, k).wait_recv()
+                xin[k] = pin[n - 2, k]
 
             weave(k, xin[k])
             last = k == chunks - 1
@@ -266,13 +261,17 @@
                     continue
                 finish(m, part)
 
+                @pl.when(helper)
+                def _():
+                    value = right_chunk(m) - sent[m]
+                    for j in range(n - 2):
+                        p_arrival(j, m).wait_recv()
+                        value = value - pin[j, m]
+                    sent[m] = value
+
                 @pl.when(lower)
                 def _():
                     p_copy(m).start()
-
-                @pl.when((r == n - 1) & (c < n - 2))
-                def _():
-                    h_copy(m).start()
 
                 for i in range(2, n):
                     @pl.when(diag & (i == r + 1))
@@ -288,11 +287,7 @@
     @pl.when(helper)
     def _():
         for k in range(chunks):
-            value = right_chunk(k) - sent[k]
-            for j in range(n - 2):
-                p_arrival(j, k).wait_recv()
-                value = value - pin[j, k]
-            weave(k, value)
+            weave(k, sent[k])
         for i in range(early):
             rows = slice(i * own, (i + 1) * own)
             part = jnp.dot(dhi[rows, :], w[...], preferred_element_type=F32)
@@ -336,11 +331,6 @@
         @pl.when(diag & ((i != r) if i >= early else ((i != r) & (r < n - 1))))
         def _():
             s_copy(i).wait_send()
-
-    @pl.when((r == n - 1) & (c < n - 2))
-    def _():
-        for m in range(chunks):
-            h_copy(m).wait_send()
 
     @pl.when(final)
     def _():
@@ -397,7 +387,6 @@
             dma,
             dma((2,)),
             dma((2,)),
-            dma((chunks,)),
         ],
         compiler_params=pltpu.CompilerParams(
             collective_id=0, has_side_effects=True, vmem_limit_bytes=40 * 1024 * 1024

time: 29.8 us -> 27.1 us (0.909)
  Pallas kernels: 29 us -> 26.3 us
    pallas_call x1, Pallas kernels: 29 us -> 26.3 us  [local(): pl.pallas_call(functools.partial(kernel, n, size, step, half), out_shape=...]
where the time goes in v4:
time: 27.1 us; the launch traced here: 26.9 us
  Pallas kernels  26.3 us (97%)
  local copies, waits for them, and re-layouts  0.63 us (2%)
    pallas_call x1, Pallas kernels, local(): pl.pallas_call(functools.partial(kernel, n, size, step, half), out_shape=...  26.3 us
    unnamed x1, local copies, waits for them, and re-layouts  0.63 us

profile of v4, /device:TPU:29, one launch (start us, length us, event | category | flops | bytes accessed | tf_op | source)
XLA Modules:
  0.0 26.9 jit_solution(6180276334815218489)
XLA Ops:
  0.0 26.3 %shard_map.37 = f32[1,64,192]{2,1,0:T(8,128)S(1)} custom-call(f32[1,1,768,768]{3,2,1,0:T(8,128)} %factor.1, f32[1,64,768]{2,1,0:T(8,128)} %bitcast.3, s32[4,4]{1,0:T(4,128)} %pattern.1), custom_call_target="tpu_custom_call" | custom-call | tf_op jit(solution)/shard_map/pallas_call | solution.py:353
  26.3 0.6 %copy.5 = f32[1,192,64]{1,2,0:T(8,128)} copy(f32[1,192,64]{1,2,0:T(8,128)S(1)} %bitcast.2) | data formatting | bytes 98304

commit v5 on v4

--- a/solution.py
+++ b/solution.py
@@ -29,7 +29,7 @@
     n, size, step, half,
     factor, rhs, pattern, out,
     links, a32, ahi, alo, right, w, acc, both, sent, xin, pin, piece, pin_slice, d32, dhi, dlo,
-    a_sem, r_sem, l_sem, x_send, x_recv, p_send, p_recv, s_send, s_recv, d_send, d_recv,
+    a_sem, r_sem, l_sem, x_send, x_recv, p_send, p_recv, s_send, s_recv, d_send, d_recv, f_send,
 ):
     r = lax.axis_index("row")
     c = lax.axis_index("col")
@@ -44,6 +44,8 @@
     final = (r == n - 1) & (c == n - 1)
     early = n // 2
     from_helper = (c == n - 1) & (r < early)
+    passes = lower & (lax.rem(r, 2) == 0) & (r < n - 1)
+    passed = (lax.rem(r, 2) == 1) & (r - 1 > c)
 
     def load(k):
         rows = pl.ds(k * step, step)
@@ -77,6 +79,10 @@
     @pl.when(jnp.logical_not(diag) & jnp.logical_not(from_helper))
     def _():
         pl.semaphore_signal(barrier, inc=1, device_id={"row": c}, device_id_type=MESH)
+
+    @pl.when(passed)
+    def _():
+        pl.semaphore_signal(barrier, inc=1, device_id={"row": r - 1}, device_id_type=MESH)
 
     @pl.when(from_helper)
     def _():
@@ -124,6 +130,12 @@
             device_id={"col": r}, device_id_type=MESH,
         )
 
+    def f_copy(m):
+        return pltpu.make_async_remote_copy(
+            src_ref=xin.at[m], dst_ref=xin.at[m], send_sem=f_send.at[m], recv_sem=x_recv.at[m],
+            device_id={"row": r + 1}, device_id_type=MESH,
+        )
+
     def d_copy(q):
         rows = pl.ds(q * part_rows, part_rows)
         return pltpu.make_async_remote_copy(
@@ -210,9 +222,13 @@
         def _():
             pl.semaphore_wait(barrier, n - 1)
 
-        @pl.when(lower & jnp.logical_not(helper))
+        @pl.when(lower & jnp.logical_not(helper) & jnp.logical_not(passes))
         def _():
             pl.semaphore_wait(barrier, 1)
+
+        @pl.when(passes)
+        def _():
+            pl.semaphore_wait(barrier, 2)
 
         @pl.when(helper)
         def _():
@@ -278,7 +294,18 @@
                     def _():
                         x_copy(i, m).start()
 
-    for i in range(2, n):
+    @pl.when(passes)
+    def _():
+        for m in range(chunks):
+            f_copy(m).start()
+
+    for i in range(1, n):
+        @pl.when(diag & (i == r + 1))
+        def _():
+            for m in range(chunks):
+                x_copy(i, m).wait_send()
+
+    for i in range(2, n, 2):
         @pl.when(diag & (i > r + 1))
         def _():
             for m in range(chunks):
@@ -323,14 +350,20 @@
             p_copy(m).wait_send()
 
     for i in range(n):
-        @pl.when(diag & (i > r))
-        def _():
-            for m in range(chunks):
-                x_copy(i, m).wait_send()
+        if i % 2 == 0:
+            @pl.when(diag & (i > r + 1))
+            def _():
+                for m in range(chunks):
+                    x_copy(i, m).wait_send()
 
         @pl.when(diag & ((i != r) if i >= early else ((i != r) & (r < n - 1))))
         def _():
             s_copy(i).wait_send()
+
+    @pl.when(passes)
+    def _():
+        for m in range(chunks):
+            f_copy(m).wait_send()
 
     @pl.when(final)
     def _():
@@ -387,6 +420,7 @@
             dma,
             dma((2,)),
             dma((2,)),
+            dma((chunks,)),
         ],
         compiler_params=pltpu.CompilerParams(
             collective_id=0, has_side_effects=True, vmem_limit_bytes=40 * 1024 * 1024

time: 27.1 us -> 27.5 us (1.015)
  Pallas kernels: 26.3 us -> 26.7 us
    pallas_call x1, Pallas kernels: 26.3 us -> 26.7 us  [local(): pl.pallas_call(functools.partial(kernel, n, size, step, half), out_shape=...]
where the time goes in v5:
time: 27.5 us; the launch traced here: 27.3 us
  Pallas kernels  26.7 us (97%)
  local copies, waits for them, and re-layouts  0.63 us (2%)
    pallas_call x1, Pallas kernels, local(): pl.pallas_call(functools.partial(kernel, n, size, step, half), out_shape=...  26.7 us
    unnamed x1, local copies, waits for them, and re-layouts  0.63 us

profile of v5, /device:TPU:29, one launch (start us, length us, event | category | flops | bytes accessed | tf_op | source)
XLA Modules:
  0.0 27.3 jit_solution(18359526555040997967)
XLA Ops:
  0.0 26.7 %shard_map.37 = f32[1,64,192]{2,1,0:T(8,128)S(1)} custom-call(f32[1,1,768,768]{3,2,1,0:T(8,128)} %factor.1, f32[1,64,768]{2,1,0:T(8,128)} %bitcast.3, s32[4,4]{1,0:T(4,128)} %pattern.1), custom_call_target="tpu_custom_call" | custom-call | tf_op jit(solution)/shard_map/pallas_call | solution.py:386
  26.7 0.6 %copy.5 = f32[1,192,64]{1,2,0:T(8,128)} copy(f32[1,192,64]{1,2,0:T(8,128)S(1)} %bitcast.2) | data formatting | bytes 98304

commit v6 on v5

--- a/solution.py
+++ b/solution.py
@@ -44,8 +44,8 @@
     final = (r == n - 1) & (c == n - 1)
     early = n // 2
     from_helper = (c == n - 1) & (r < early)
-    passes = lower & (lax.rem(r, 2) == 0) & (r < n - 1)
-    passed = (lax.rem(r, 2) == 1) & (r - 1 > c)
+    passes = lower & (lax.rem(r, 2) == 0) & (r < n - 1) & (c > 0)
+    passed = (lax.rem(r, 2) == 1) & (r - 1 > c) & (c > 0)
 
     def load(k):
         rows = pl.ds(k * step, step)
@@ -305,8 +305,8 @@
             for m in range(chunks):
                 x_copy(i, m).wait_send()
 
-    for i in range(2, n, 2):
-        @pl.when(diag & (i > r + 1))
+    for i in range(2, n):
+        @pl.when(diag & (i > r + 1) & ((r == 0) | (i % 2 == 0)))
         def _():
             for m in range(chunks):
                 x_copy(i, m).start()
@@ -350,11 +350,10 @@
             p_copy(m).wait_send()
 
     for i in range(n):
-        if i % 2 == 0:
-            @pl.when(diag & (i > r + 1))
-            def _():
-                for m in range(chunks):
-                    x_copy(i, m).wait_send()
+        @pl.when(diag & (i > r + 1) & ((r == 0) | (i % 2 == 0)))
+        def _():
+            for m in range(chunks):
+                x_copy(i, m).wait_send()
 
         @pl.when(diag & ((i != r) if i >= early else ((i != r) & (r < n - 1))))
         def _():

time: 27.5 us -> 26.8 us (0.975)
  Pallas kernels: 26.7 us -> 26 us
    pallas_call x1, Pallas kernels: 26.7 us -> 26 us  [local(): pl.pallas_call(functools.partial(kernel, n, size, step, half), out_shape=...]
where the time goes in v6:
time: 26.8 us; the launch traced here: 26.6 us
  Pallas kernels  26 us (97%)
  local copies, waits for them, and re-layouts  0.63 us (2%)
    pallas_call x1, Pallas kernels, local(): pl.pallas_call(functools.partial(kernel, n, size, step, half), out_shape=...  26 us
    unnamed x1, local copies, waits for them, and re-layouts  0.63 us

profile of v6, /device:TPU:29, one launch (start us, length us, event | category | flops | bytes accessed | tf_op | source)
XLA Modules:
  0.0 26.6 jit_solution(6646766290513901249)
XLA Ops:
  0.0 26.0 %shard_map.37 = f32[1,64,192]{2,1,0:T(8,128)S(1)} custom-call(f32[1,1,768,768]{3,2,1,0:T(8,128)} %factor.1, f32[1,64,768]{2,1,0:T(8,128)} %bitcast.3, s32[4,4]{1,0:T(4,128)} %pattern.1), custom_call_target="tpu_custom_call" | custom-call | tf_op jit(solution)/shard_map/pallas_call | solution.py:385
  26.0 0.6 %copy.5 = f32[1,192,64]{1,2,0:T(8,128)} copy(f32[1,192,64]{1,2,0:T(8,128)S(1)} %bitcast.2) | data formatting | bytes 98304

commit v7 on v6

--- a/solution.py
+++ b/solution.py
@@ -203,7 +203,8 @@
             finish(m, product(slice(m * step, (m + 1) * step), slice(0, size)))
             if m == 0:
                 pl.semaphore_wait(barrier, n - 1)
-            x_copy(1, m).start()
+            for i in range(1, n):
+                x_copy(i, m).start()
 
     @pl.when(active & (r > 0))
     def _():
@@ -305,8 +306,8 @@
             for m in range(chunks):
                 x_copy(i, m).wait_send()
 
-    for i in range(2, n):
-        @pl.when(diag & (i > r + 1) & ((r == 0) | (i % 2 == 0)))
+    for i in range(4, n, 2):
+        @pl.when(diag & (i > r + 1) & (r > 0))
         def _():
             for m in range(chunks):
                 x_copy(i, m).start()

time: 26.8 us -> 26.3 us (0.981)
  Pallas kernels: 26 us -> 25.6 us
    pallas_call x1, Pallas kernels: 26 us -> 25.6 us  [local(): pl.pallas_call(functools.partial(kernel, n, size, step, half), out_shape=...]
where the time goes in v7:
time: 26.3 us; the launch traced here: 26.2 us
  Pallas kernels  25.6 us (97%)
  local copies, waits for them, and re-layouts  0.63 us (2%)
    pallas_call x1, Pallas kernels, local(): pl.pallas_call(functools.partial(kernel, n, size, step, half), out_shape=...  25.6 us
    unnamed x1, local copies, waits for them, and re-layouts  0.63 us

profile of v7, /device:TPU:29, one launch (start us, length us, event | category | flops | bytes accessed | tf_op | source)
XLA Modules:
  0.0 26.2 jit_solution(4202022833021581128)
XLA Ops:
  0.0 25.6 %shard_map.37 = f32[1,64,192]{2,1,0:T(8,128)S(1)} custom-call(f32[1,1,768,768]{3,2,1,0:T(8,128)} %factor.1, f32[1,64,768]{2,1,0:T(8,128)} %bitcast.3, s32[4,4]{1,0:T(4,128)} %pattern.1), custom_call_target="tpu_custom_call" | custom-call | tf_op jit(solution)/shard_map/pallas_call | solution.py:386
  25.6 0.6 %copy.5 = f32[1,192,64]{1,2,0:T(8,128)} copy(f32[1,192,64]{1,2,0:T(8,128)S(1)} %bitcast.2) | data formatting | bytes 98304

commit v8 on v7

--- a/solution.py
+++ b/solution.py
@@ -57,19 +57,6 @@
     def load_links():
         return pltpu.make_async_copy(pattern, links, l_sem)
 
-    @pl.when(active)
-    def _():
-        load_links().start()
-
-    @pl.when(diag | helper)
-    def _():
-        load_right().start()
-
-    @pl.when(active)
-    def _():
-        for k in range(chunks):
-            load(k).start()
-
     barrier = pltpu.get_barrier_semaphore()
     for i in range(n):
         @pl.when(diag & (i < r) & ((r < n - 1) | (i == n - 2)))
@@ -95,6 +82,19 @@
         for j in range(n):
             if j != n - 2:
                 pl.semaphore_signal(barrier, inc=1, device_id={"col": j}, device_id_type=MESH)
+
+    @pl.when(active)
+    def _():
+        load_links().start()
+
+    @pl.when(diag | helper)
+    def _():
+        load_right().start()
+
+    @pl.when(active)
+    def _():
+        for k in range(chunks):
+            load(k).start()
 
     block = 64
     part_rows = early * own // 2

time: 26.3 us -> 26.3 us (level)
  no operation moved by 1% of the time
where the time goes in v8:
time: 26.3 us; the launch traced here: 26.2 us
  Pallas kernels  25.6 us (97%)
  local copies, waits for them, and re-layouts  0.63 us (2%)
    pallas_call x1, Pallas kernels, local(): pl.pallas_call(functools.partial(kernel, n, size, step, half), out_shape=...  25.6 us
    unnamed x1, local copies, waits for them, and re-layouts  0.63 us

profile of v8, /device:TPU:29, one launch (start us, length us, event | category | flops | bytes accessed | tf_op | source)
XLA Modules:
  0.0 26.2 jit_solution(1893246260391749908)
XLA Ops:
  0.0 25.6 %shard_map.37 = f32[1,64,192]{2,1,0:T(8,128)S(1)} custom-call(f32[1,1,768,768]{3,2,1,0:T(8,128)} %factor.1, f32[1,64,768]{2,1,0:T(8,128)} %bitcast.3, s32[4,4]{1,0:T(4,128)} %pattern.1), custom_call_target="tpu_custom_call" | custom-call | tf_op jit(solution)/shard_map/pallas_call | solution.py:386
  25.6 0.6 %copy.5 = f32[1,192,64]{1,2,0:T(8,128)} copy(f32[1,192,64]{1,2,0:T(8,128)S(1)} %bitcast.2) | data formatting | bytes 98304
